TPU v7x, 256 devices: a whole 4x4x8 slice. The times are simulated.
256 devices in a mesh: dp: 32 (over x, z_hi, core), expert: 8 (over y, z_lo).
Axes of the slice: x: 4, y: 4, z: 8 (z_hi: 4, z_lo: 2; z = z_hi * 2 + z_lo), core: 2. Of those that a mesh axis runs over, the one named last changes fastest.
Arguments:
- tokens: bfloat16 [32768, 4096], P(('dp', 'expert')), may hold values from -6 to 6
- cotangent: bfloat16 [32768, 4096], P(('dp', 'expert')), may hold values from -1.1953125 to 1.1953125
- expert_ids: int32 [32768, 2], P(('dp', 'expert')), may hold values from 0 to 63, as said below
- gate_probs: bfloat16 [32768, 2], P(('dp', 'expert')), may hold values from 0.049804688 to 1
- gate_w: bfloat16 [8, 7168, 4096], P('expert', 'dp'), may hold values from -0.09375 to 0.09375
- up_w: bfloat16 [8, 7168, 4096], P('expert', 'dp'), may hold values from -0.09375 to 0.09375
- down_w: bfloat16 [8, 7168, 4096], P('expert', 'dp'), may hold values from -0.0625 to 0.0625
Outputs:
- grad_gate: bfloat16 [8, 7168, 4096], P('expert', 'dp')
- grad_up: bfloat16 [8, 7168, 4096], P('expert', 'dp')
- grad_down: bfloat16 [8, 7168, 4096], P('expert', 'dp')
- grad_probs: float32 [32768, 2], P(('dp', 'expert'))
Inputs may be any that keep to these rules, and one draw needn't show every extreme that they name: `expert_ids`: each token names two different experts. Split the rows into aligned blocks of 128 (the rows of one device) and those into aligned runs of 8 blocks: a block names any one expert below 8 at most 4 times, and a run names it at most 16 times; in every draw some block reaches 4 and some run reaches 16.
All inputs are finite; a program needn't handle non-finite values.
Results may differ from a plain program's by a relative error of at most 0.015.
Values may be sent and summed in bfloat16 or wider, within the bound.
No kernel may reach another device: no remote copies, remote signals or barrier semaphores. Data moves between devices by JAX's collectives and lax.ppermute only.
A program may use at most 128 MiB of HBM per device.

v0:
```python
import jax
import jax.numpy as jnp
from jax import lax
from jax.sharding import PartitionSpec as P

ROW_CAPACITY = 4


def contract_rows(left, right):
    return lax.dot_general(
        left, right, (((0,), (0,)), ((), ())), preferred_element_type=jnp.float32
    )


def contract_cols(left, right):
    return lax.dot_general(
        left, right, (((1,), (1,)), ((), ())), preferred_element_type=jnp.float32
    )


def shards(tokens, cotangent, expert_ids, gate_probs, gate_w, up_w, down_w):
    owners = lax.axis_size("expert")
    slots = owners * ROW_CAPACITY
    flat_ids = expert_ids.reshape(-1)
    marks = (flat_ids[:, None] == jnp.arange(owners, dtype=jnp.int32)[None, :]).astype(jnp.int32)
    before = jnp.cumsum(marks, axis=0) - marks
    ranking = jnp.sum(before * marks, axis=1)
    target = jnp.where(jnp.sum(marks, axis=1) > 0, flat_ids * ROW_CAPACITY + ranking, -1)
    routing = (target[None, :] == jnp.arange(slots, dtype=jnp.int32)[:, None]).astype(jnp.float32)
    per_token = routing.reshape(slots, -1, 2).sum(axis=2).astype(jnp.bfloat16)
    send_x = jnp.dot(per_token, tokens, preferred_element_type=jnp.float32).astype(jnp.bfloat16)
    send_dy = jnp.dot(per_token, cotangent, preferred_element_type=jnp.float32).astype(jnp.bfloat16)
    send_p = jnp.dot(
        routing.astype(jnp.bfloat16), gate_probs.reshape(-1), preferred_element_type=jnp.float32
    ).astype(jnp.bfloat16)
    got_x, got_dy, got_p = (
        lax.all_to_all(
            send_x.reshape(owners, ROW_CAPACITY, -1),
            "expert",
            split_axis=0,
            concat_axis=0,
            tiled=True,
        ),
        lax.all_to_all(
            send_dy.reshape(owners, ROW_CAPACITY, -1),
            "expert",
            split_axis=0,
            concat_axis=0,
            tiled=True,
        ),
        lax.all_to_all(
            send_p.reshape(owners, ROW_CAPACITY), "expert", split_axis=0, concat_axis=0, tiled=True
        ),
    )
    rows_x = got_x.reshape(slots, -1)
    rows_dy = got_dy.reshape(slots, -1)
    rows_p = got_p.reshape(slots)
    gate_local = gate_w[0]
    up_local = up_w[0]
    down_local = down_w[0]
    piece_x = lax.all_gather(rows_x, "dp", axis=0, tiled=True)
    piece_dy = lax.all_gather(rows_dy, "dp", axis=0, tiled=True)
    piece_p = lax.all_gather(rows_p, "dp", axis=0, tiled=True)
    weight_p = piece_p.astype(jnp.float32)[:, None]
    gate_pre = contract_cols(piece_x, gate_local)
    up_pre = contract_cols(piece_x, up_local)
    sigma = jax.nn.sigmoid(gate_pre)
    hidden = (gate_pre * sigma * up_pre).astype(jnp.bfloat16)
    pulled = contract_cols(piece_dy, down_local)
    router = jnp.sum(hidden.astype(jnp.float32) * pulled, axis=1)
    scaled_dy = (weight_p * piece_dy.astype(jnp.float32)).astype(jnp.bfloat16)
    d_hidden = weight_p * pulled
    d_gate = (d_hidden * up_pre * sigma * (1.0 + gate_pre * (1.0 - sigma))).astype(jnp.bfloat16)
    d_up = (d_hidden * gate_pre * sigma).astype(jnp.bfloat16)
    new_gate = contract_rows(d_gate, piece_x)
    new_up = contract_rows(d_up, piece_x)
    new_down = contract_rows(hidden, scaled_dy)
    router_rows = lax.psum_scatter(router, "dp", scatter_dimension=0, tiled=True)
    returned = lax.all_to_all(
        router_rows.reshape(owners, ROW_CAPACITY), "expert", split_axis=0, concat_axis=0, tiled=True
    )
    grad_flat = jnp.dot(returned.reshape(slots), routing, precision=lax.Precision.HIGHEST)
    grad_gate = new_gate.astype(jnp.bfloat16)[None]
    grad_up = new_up.astype(jnp.bfloat16)[None]
    grad_down = new_down.astype(jnp.bfloat16)[None]
    return (grad_gate, grad_up, grad_down, grad_flat.reshape(-1, 2))


def solution(mesh):
    in_specs = (
        P(("dp", "expert"), None),
        P(("dp", "expert"), None),
        P(("dp", "expert"), None),
        P(("dp", "expert"), None),
        P("expert", "dp", None),
        P("expert", "dp", None),
        P("expert", "dp", None),
    )
    out_specs = (
        P("expert", "dp", None),
        P("expert", "dp", None),
        P("expert", "dp", None),
        P(("dp", "expert"), None),
    )
    return jax.shard_map(shards, mesh=mesh, in_specs=in_specs, out_specs=out_specs, check_vma=False)
```

profile of v0, /device:TPU:8, one launch (start us, length us, event | category | flops | bytes accessed | tf_op | source)
XLA Modules:
  0.0 299.6 jit_solution(5309269911778163074)
XLA Ops:
  7.2 0.9 copy.36
  9.8 0.7 add_select_fusion
  10.6 1.5 convolution_convert_fusion.2
  12.2 11.8 %all_to_all.29 = bf16[8,4,4096]{2,1,0:T(4,128)(2,1)S(1)} all-to-all(bf16[8,4,4096]{2,1,0:T(4,128)(2,1)S(1)} %reshape.108), channel_id=1, replica_groups=mesh['dp'=32,'expert'=8] {'expert'}, dimensions={0} | all-to-all | bytes 524288 | tf_op jit(solution)/shard_map/all_to_all | solution.py:37
  24.0 0.8 reshape.109
  24.8 1.5 convolution_convert_fusion.3
  26.5 9.6 %all_to_all.30 = bf16[8,4,4096]{2,1,0:T(4,128)(2,1)S(1)} all-to-all(bf16[8,4,4096]{2,1,0:T(4,128)(2,1)S(1)} %reshape.106), channel_id=1, replica_groups=mesh['dp'=32,'expert'=8] {'expert'}, dimensions={0} | all-to-all | bytes 524288 | tf_op jit(solution)/shard_map/all_to_all | solution.py:44
  36.0 0.8 reshape.107
  36.8 0.8 copy.38
  37.9 0.7 all_to_all.24
  38.6 5.0 %all-to-all-start = ((bf16[8,1,4]{2,1,0:T(2,128)(2,1)}), bf16[8,1,4]{2,1,0:T(2,128)(2,1)S(1)}, u32[]{:S(2)}, u32[]{:S(2)}) async-start(bf16[8,1,4]{2,1,0:T(2,128)(2,1)} %all_to_all.24), calls=%async_computation | async-start | bytes 8192 | tf_op jit(solution)/shard_map/all_to_all | solution.py:51
  43.6 1.3 fusion.29
  46.1 2.1 all-to-all-done
  48.6 77.6 %all-reduce = bf16[1024]{0:T(1024)(128)(2,1)S(1)} all-reduce(bf16[1024]{0:T(1024)(128)(2,1)S(1)} %dynamic-update-slice), channel_id=1, replica_groups=mesh['dp'=32,'expert'=8] {'dp'}, use_global_device_ids=true, to_apply=%add | all-reduce | flops 1024 | bytes 4096
  126.2 6.8 %fusion.6 = f32[1024,224]{0,1:T(8,128)S(1)} fusion(bf16[1024,4096]{1,0:T(8,128)(2,1)} %all-gather.5.cloned.1.call-done, bf16[1,224,4096]{2,1,0:T(8,128)(2,1)} %param.11), kind=kOutput, calls=%fused_computation.11 | convolution fusion | flops 1879048192 | bytes 11141120 | tf_op jit(solution)/shard_map/dot_general | solution.py:16
  133.1 3.6 %fusion.8 = f32[1024,224]{0,1:T(8,128)} fusion(bf16[1024,4096]{1,0:T(8,128)(2,1)S(1)} %copy-done.1, bf16[1,224,4096]{2,1,0:T(8,128)(2,1)S(1)} %copy-done.3), kind=kOutput, calls=%fused_computation.13 | convolution fusion | flops 1879048192 | bytes 11141120 | tf_op jit(solution)/shard_map/dot_general | solution.py:16
  136.7 48.4 %all-gather.3.cloned.1.call-done = bf16[1024,4096]{1,0:T(8,128)(2,1)} async-done(((bf16[32,4096]{1,0:T(8,128)(2,1)}), bf16[1024,4096]{1,0:T(8,128)(2,1)}) %all-gather.3.cloned.1.call-update) | async-done | bytes 8388624 | tf_op jit(solution)/shard_map/all_gather | solution.py:62
  185.1 7.2 %multiply_reduce_fusion = (f32[1024]{0:T(1024)S(1)}, bf16[1024,224]{0,1:T(8,128)(2,1)S(1)}, f32[1024,224]{0,1:T(8,128)}) fusion(f32[1024,224]{0,1:T(8,128)} %fusion.8, f32[1024,224]{0,1:T(8,128)S(1)} %fusion.6, bf16[1024,4096]{1,0:T(8,128)(2,1)} %all-gather.3.cloned.1.call-done, bf16[1,224,4096]{2,1,0:T(8,128)(2,1)S(1)} %copy-done), kind=kOutput, calls=%fused_computation.19 | convolution fusion | flops 1881111552 | bytes 13438976 | tf_op jit(solution)/shard_map/dot_general | solution.py:16
  192.3 75.1 %all-reduce.1 = f32[1024]{0:T(1024)S(1)} all-reduce(f32[1024]{0:T(1024)S(1)} %get-tuple-element.6), channel_id=2, replica_groups=mesh['dp'=32,'expert'=8] {'dp'}, use_global_device_ids=true, to_apply=%region_6.7.clone | all-reduce | flops 1024 | bytes 8192
  268.1 4.8 %all-to-all-start.3 = ((f32[8,1,4]{2,1,0:T(1,128)}), f32[8,1,4]{2,1,0:T(1,128)S(1)}, u32[]{:S(2)}, u32[]{:S(2)}) async-start(f32[8,1,4]{2,1,0:T(1,128)} %bitcast.10), calls=%async_computation.3 | async-start | bytes 8192 | tf_op jit(solution)/shard_map/all_to_all | solution.py:79
  272.9 7.5 %fusion.3 = bf16[1,224,4096]{2,1,0:T(8,128)(2,1)} fusion(bf16[1024,4096]{1,0:T(8,128)(2,1)} %all-gather.5.cloned.1.call-done, f32[1024,224]{0,1:T(8,128)S(1)} %fusion.6, f32[1024,224]{0,1:T(8,128)} %fusion.8, f32[1024,224]{0,1:T(8,128)} %get-tuple-element.12, f32[1024]{0:T(1024)S(1)} %convert_element_type.63), kind=kOutput, calls=%fused_computation.6 | convolution fusion | flops 1882488832 | bytes 12980224 | tf_op jit(solution)/shard_map/dot_general | solution.py:10
  280.4 6.9 %fusion.4 = bf16[1,224,4096]{2,1,0:T(8,128)(2,1)} fusion(bf16[1024,4096]{1,0:T(8,128)(2,1)} %all-gather.5.cloned.1.call-done, f32[1024,224]{0,1:T(8,128)S(1)} %fusion.6, f32[1024,224]{0,1:T(8,128)S(1)} %copy-done.4, f32[1024]{0:T(1024)S(1)} %convert_element_type.63), kind=kOutput, calls=%fused_computation.7 | convolution fusion | flops 1881571328 | bytes 12062720 | tf_op jit(solution)/shard_map/dot_general | solution.py:10
  287.3 3.5 %fusion.5 = bf16[1,224,4096]{2,1,0:T(8,128)(2,1)} fusion(bf16[1024,224]{0,1:T(8,128)(2,1)S(1)} %get-tuple-element.7, bf16[1024,4096]{1,0:T(8,128)(2,1)S(1)} %copy-done.2, f32[1024]{0:T(1024)S(1)} %convert_element_type.63), kind=kOutput, calls=%fused_computation.8 | convolution fusion | flops 1892548608 | bytes 10686464 | tf_op jit(solution)/shard_map/dot_general | solution.py:10
  292.1 0.7 fusion.18
  (44 shorter events, 4.8 us)
Async XLA Ops:
  7.2 177.9 %copy-start = (bf16[1,224,4096]{2,1,0:T(8,128)(2,1)S(1)}, bf16[1,224,4096]{2,1,0:T(8,128)(2,1)}, u32[]{:S(2)}) copy-start(bf16[1,224,4096]{2,1,0:T(8,128)(2,1)} %param.13) | copy-start | bytes 5505028
  7.2 119.0 %all-gather.5.cloned.1.call-start = ((), (), s32[]{:S(2)}) async-start(), calls=%async_computation.5 | async-start | bytes 8650752 | tf_op jit(solution)/shard_map/all_gather | solution.py:61
  24.8 160.3 %all-gather.3.cloned.1.call-start = ((), (), s32[]{:S(2)}) async-start(), calls=%async_computation.4 | async-start | bytes 8650752 | tf_op jit(solution)/shard_map/all_gather | solution.py:62
  38.6 9.7 %all-to-all-start = ((bf16[8,1,4]{2,1,0:T(2,128)(2,1)}), bf16[8,1,4]{2,1,0:T(2,128)(2,1)S(1)}, u32[]{:S(2)}, u32[]{:S(2)}) async-start(bf16[8,1,4]{2,1,0:T(2,128)(2,1)} %all_to_all.24), calls=%async_computation | async-start | bytes 8192 | tf_op jit(solution)/shard_map/all_to_all | solution.py:51
  126.2 6.8 %copy-start.1 = (bf16[1024,4096]{1,0:T(8,128)(2,1)S(1)}, bf16[1024,4096]{1,0:T(8,128)(2,1)}, u32[]{:S(2)}) copy-start(bf16[1024,4096]{1,0:T(8,128)(2,1)} %all-gather.5.cloned.1.call-done) | copy-start | bytes 25165828
  126.2 6.9 %copy-start.3 = (bf16[1,224,4096]{2,1,0:T(8,128)(2,1)S(1)}, bf16[1,224,4096]{2,1,0:T(8,128)(2,1)}, u32[]{:S(2)}) copy-start(bf16[1,224,4096]{2,1,0:T(8,128)(2,1)} %param.12) | copy-start | bytes 5505028
  268.1 22.7 %all-to-all-start.3 = ((f32[8,1,4]{2,1,0:T(1,128)}), f32[8,1,4]{2,1,0:T(1,128)S(1)}, u32[]{:S(2)}, u32[]{:S(2)}) async-start(f32[8,1,4]{2,1,0:T(1,128)} %bitcast.10), calls=%async_computation.3 | async-start | bytes 8192 | tf_op jit(solution)/shard_map/all_to_all | solution.py:79
  272.9 7.5 %copy-start.4 = (f32[1024,224]{0,1:T(8,128)S(1)}, f32[1024,224]{0,1:T(8,128)}, u32[]{:S(2)}) copy-start(f32[1024,224]{0,1:T(8,128)} %get-tuple-element.12) | copy-start | bytes 2752516
  280.4 6.9 %copy-start.2 = (bf16[1024,4096]{1,0:T(8,128)(2,1)S(1)}, bf16[1024,4096]{1,0:T(8,128)(2,1)}, u32[]{:S(2)}) copy-start(bf16[1024,4096]{1,0:T(8,128)(2,1)} %all-gather.3.cloned.1.call-done) | copy-start | bytes 25165828
Sparse Core Ops, SparseCore 0:
  24.9 79.0 all-gather.4
  107.1 77.8 all-gather.2
where the time goes:
time: 300 us
  blocking collectives  174 us (58%)
  waiting for transfers between devices  50.6 us (17%)
  matrix products  39.2 us (13%)
  between operations  15.4 us (5%)
  starting transfers between devices  9.87 us (3%)
  local copies, waits for them, and re-layouts  8.39 us (3%)
    unnamed x2, blocking collectives  153 us
    all_gather x1, waiting for transfers between devices, shards(): piece_dy = lax.all_gather(rows_dy, 'dp', axis=0, tiled=True)  48.4 us
    dot_general x3, matrix products, contract_rows(): lax.dot_general(left, right, (((0,), (0,)), ((), ())), preferred_element_...  17.9 us
    dot_general x3, matrix products, contract_cols(): lax.dot_general(left, right, (((1,), (1,)), ((), ())), preferred_element_...  17.5 us
    all_to_all x1, blocking collectives, shards(): lax.all_to_all(send_x.reshape(owners, ROW_CAPACITY, -1), 'expert', split_...  11.8 us
    all_to_all x1, blocking collectives, shards(): lax.all_to_all(send_dy.reshape(owners, ROW_CAPACITY, -1), 'expert', split...  9.57 us
  transfers between devices with their start and end apart: 4, of which 2 were waited for; matrix products, arithmetic and copies ran while one was open for 11% of the time, Pallas kernels for 0%

commit v1 on v0

--- a/solution.py
+++ b/solution.py
@@ -59,7 +59,9 @@
     up_local = up_w[0]
     down_local = down_w[0]
     piece_x = lax.all_gather(rows_x, "dp", axis=0, tiled=True)
-    piece_dy = lax.all_gather(rows_dy, "dp", axis=0, tiled=True)
+    piece_dy = jnp.concatenate(
+        lax.all_to_all(jnp.stack([rows_dy] * lax.axis_size("dp")), "dp", 0, 0), axis=0
+    )
     piece_p = lax.all_gather(rows_p, "dp", axis=0, tiled=True)
     weight_p = piece_p.astype(jnp.float32)[:, None]
     gate_pre = contract_cols(piece_x, gate_local)

time: 300 us -> 469 us (1.56)
  blocking collectives: 174 us -> 363 us
  waiting for transfers between devices: 50.6 us -> 8.39 us
  starting transfers between devices: 9.87 us -> 25.5 us
    unnamed x2, blocking collectives: 153 us -> 351 us
    all_gather x1 -> x0, waiting for transfers between devices: 48.4 us -> none  [shards(): piece_dy = lax.all_gather(rows_dy, 'dp', axis=0, tiled=True)]
    all_to_all x0 -> x2, starting transfers between devices: none -> 15.5 us  [the longest x1 10.7 us: shards(): lax.all_to_all(jnp.stack([rows_dy] * lax.axis_size('dp')), 'dp', 0, 0)]
    all_to_all x1 -> x0, blocking collectives: 9.57 us -> none  [shards(): lax.all_to_all(send_dy.reshape(owners, ROW_CAPACITY, -1), 'expert', split...]
  transfers between devices with their start and end apart: 4 -> 5, of which waited for: 2 -> 2; matrix products, arithmetic and copies ran while one was open for 11% -> 8% of each run, Pallas kernels for 0% -> 0%
where the time goes in v1:
time: 469 us; the launch traced here: 468 us
  blocking collectives  363 us (77%)
  matrix products  42.1 us (9%)
  starting transfers between devices  25.5 us (5%)
  between operations  15.5 us (3%)
  local copies, waits for them, and re-layouts  11.9 us (3%)
  waiting for transfers between devices  8.39 us (2%)
    unnamed x2, blocking collectives  351 us
    dot_general x3, matrix products, contract_rows(): lax.dot_general(left, right, (((0,), (0,)), ((), ())), preferred_element_...  20.8 us
    dot_general x3, matrix products, contract_cols(): lax.dot_general(left, right, (((1,), (1,)), ((), ())), preferred_element_...  17.4 us
    all_to_all x1, blocking collectives, shards(): lax.all_to_all(send_x.reshape(owners, ROW_CAPACITY, -1), 'expert', split_...  11.8 us
    all_to_all x1, starting transfers between devices, shards(): lax.all_to_all(jnp.stack([rows_dy] * lax.axis_size('dp')), 'dp', 0, 0)  10.7 us
  transfers between devices with their start and end apart: 5, of which 2 were waited for; matrix products, arithmetic and copies ran while one was open for 8% of the time, Pallas kernels for 0%

profile of v1, /device:TPU:8, one launch (start us, length us, event | category | flops | bytes accessed | tf_op | source)
XLA Modules:
  0.0 468.0 jit_solution(15662143099130076043)
XLA Ops:
  7.2 0.9 copy.36
  9.8 0.7 add_select_fusion
  10.6 1.5 convolution_convert_fusion.2
  12.2 11.8 %all_to_all.34 = bf16[8,4,4096]{2,1,0:T(4,128)(2,1)S(1)} all-to-all(bf16[8,4,4096]{2,1,0:T(4,128)(2,1)S(1)} %reshape.110), channel_id=1, replica_groups=mesh['dp'=32,'expert'=8] {'expert'}, dimensions={0} | all-to-all | bytes 524288 | tf_op jit(solution)/shard_map/all_to_all | solution.py:37
  24.0 0.8 reshape.111
  24.8 1.5 convolution_convert_fusion.3
  26.3 0.8 reshape.108
  27.1 4.8 %all-to-all-start.1 = ((bf16[8,4,4096]{2,1,0:T(4,128)(2,1)}), bf16[8,4,4096]{2,1,0:T(4,128)(2,1)S(1)}, u32[]{:S(2)}, u32[]{:S(2)}) async-start(bf16[8,4,4096]{2,1,0:T(4,128)(2,1)} %reshape.108), calls=%async_computation.1 | async-start | bytes 524288 | tf_op jit(solution)/shard_map/all_to_all | solution.py:44
  32.0 0.8 copy.38
  33.0 0.7 all_to_all.28
  33.7 3.8 all-to-all-done.1
  37.5 5.0 %all-to-all-start = ((bf16[8,1,4]{2,1,0:T(2,128)(2,1)}), bf16[8,1,4]{2,1,0:T(2,128)(2,1)S(1)}, u32[]{:S(2)}, u32[]{:S(2)}) async-start(bf16[8,1,4]{2,1,0:T(2,128)(2,1)} %all_to_all.28), calls=%async_computation | async-start | bytes 8192 | tf_op jit(solution)/shard_map/all_to_all | solution.py:51
  42.6 4.6 all-to-all-done
  47.2 4.3 stack.3
  51.4 10.7 %all-to-all-start.2 = ((bf16[32,32,4096]{2,1,0:T(8,128)(2,1)}), bf16[32,32,4096]{2,1,0:T(8,128)(2,1)}, u32[]{:S(2)}, u32[]{:S(2)}) async-start(bf16[32,32,4096]{2,1,0:T(8,128)(2,1)} %stack.3), calls=%async_computation.2 | async-start | bytes 16777216 | tf_op jit(solution)/shard_map/all_to_all | solution.py:63
  64.4 280.9 %all-reduce = bf16[1024]{0:T(1024)(128)(2,1)S(1)} all-reduce(bf16[1024]{0:T(1024)(128)(2,1)S(1)} %dynamic-update-slice), channel_id=1, replica_groups=mesh['dp'=32,'expert'=8] {'dp'}, use_global_device_ids=true, to_apply=%add | all-reduce | flops 1024 | bytes 4096
  345.3 6.7 %fusion.6 = f32[1024,224]{0,1:T(8,128)S(1)} fusion(bf16[1024,4096]{1,0:T(8,128)(2,1)} %all-gather.2.cloned.1.call-done, bf16[1,224,4096]{2,1,0:T(8,128)(2,1)} %param.11), kind=kOutput, calls=%fused_computation.11 | convolution fusion | flops 1879048192 | bytes 11141120 | tf_op jit(solution)/shard_map/dot_general | solution.py:16
  352.1 3.6 fusion.8
  355.7 7.2 %multiply_reduce_fusion = (f32[1024]{0:T(1024)S(1)}, bf16[1024,224]{0,1:T(8,128)(2,1)S(1)}, f32[1024,224]{0,1:T(8,128)}) fusion(f32[1024,224]{0,1:T(8,128)} %fusion.8, f32[1024,224]{0,1:T(8,128)S(1)} %fusion.6, bf16[1024,4096]{1,0:T(8,128)(2,1)} %bitcast.4, bf16[1,224,4096]{2,1,0:T(8,128)(2,1)S(1)} %copy-done), kind=kOutput, calls=%fused_computation.19 | convolution fusion | flops 1881111552 | bytes 13438976 | tf_op jit(solution)/shard_map/dot_general | solution.py:16
  362.8 69.9 %all-reduce.1 = f32[1024]{0:T(1024)S(1)} all-reduce(f32[1024]{0:T(1024)S(1)} %get-tuple-element.6), channel_id=2, replica_groups=mesh['dp'=32,'expert'=8] {'dp'}, use_global_device_ids=true, to_apply=%region_6.7.clone | all-reduce | flops 1024 | bytes 8192
  433.4 4.9 %all-to-all-start.4 = ((f32[8,1,4]{2,1,0:T(1,128)}), f32[8,1,4]{2,1,0:T(1,128)S(1)}, u32[]{:S(2)}, u32[]{:S(2)}) async-start(f32[8,1,4]{2,1,0:T(1,128)} %bitcast.11), calls=%async_computation.4 | async-start | bytes 8192 | tf_op jit(solution)/shard_map/all_to_all | solution.py:81
  438.4 7.2 %fusion.4 = bf16[1,224,4096]{2,1,0:T(8,128)(2,1)} fusion(bf16[1024,4096]{1,0:T(8,128)(2,1)} %all-gather.2.cloned.1.call-done, f32[1024,224]{0,1:T(8,128)S(1)} %fusion.6, f32[1024,224]{0,1:T(8,128)} %get-tuple-element.12, f32[1024]{0:T(1024)S(1)} %convert_element_type.63), kind=kOutput, calls=%fused_computation.7 | convolution fusion | flops 1881571328 | bytes 12062720 | tf_op jit(solution)/shard_map/dot_general | solution.py:10
  445.5 6.9 %fusion.3 = bf16[1,224,4096]{2,1,0:T(8,128)(2,1)} fusion(bf16[1024,4096]{1,0:T(8,128)(2,1)} %all-gather.2.cloned.1.call-done, f32[1024,224]{0,1:T(8,128)S(1)} %fusion.6, f32[1024,224]{0,1:T(8,128)S(1)} %copy-done.4, f32[1024,224]{0,1:T(8,128)S(1)} %copy-done.5, f32[1024]{0:T(1024)S(1)} %convert_element_type.63), kind=kOutput, calls=%fused_computation.6 | convolution fusion | flops 1882488832 | bytes 12980224 | tf_op jit(solution)/shard_map/dot_general | solution.py:10
  452.4 6.8 %fusion.5 = bf16[1,224,4096]{2,1,0:T(8,128)(2,1)} fusion(bf16[1024,224]{0,1:T(8,128)(2,1)S(1)} %get-tuple-element.7, bf16[1024,4096]{1,0:T(8,128)(2,1)} %bitcast.4, f32[1024]{0:T(1024)S(1)} %convert_element_type.63), kind=kOutput, calls=%fused_computation.8 | convolution fusion | flops 1892548608 | bytes 10686464 | tf_op jit(solution)/shard_map/dot_general | solution.py:10
  (47 shorter events, 5.9 us)
Async XLA Ops:
  7.2 348.5 %copy-start = (bf16[1,224,4096]{2,1,0:T(8,128)(2,1)S(1)}, bf16[1,224,4096]{2,1,0:T(8,128)(2,1)}, u32[]{:S(2)}) copy-start(bf16[1,224,4096]{2,1,0:T(8,128)(2,1)} %param.13) | copy-start | bytes 5505028
  7.2 338.1 %all-gather.2.cloned.1.call-start = ((), (), s32[]{:S(2)}) async-start(), calls=%async_computation.5 | async-start | bytes 8650752 | tf_op jit(solution)/shard_map/all_gather | solution.py:61
  27.1 10.4 %all-to-all-start.1 = ((bf16[8,4,4096]{2,1,0:T(4,128)(2,1)}), bf16[8,4,4096]{2,1,0:T(4,128)(2,1)S(1)}, u32[]{:S(2)}, u32[]{:S(2)}) async-start(bf16[8,4,4096]{2,1,0:T(4,128)(2,1)} %reshape.108), calls=%async_computation.1 | async-start | bytes 524288 | tf_op jit(solution)/shard_map/all_to_all | solution.py:44
  37.5 9.7 %all-to-all-start = ((bf16[8,1,4]{2,1,0:T(2,128)(2,1)}), bf16[8,1,4]{2,1,0:T(2,128)(2,1)S(1)}, u32[]{:S(2)}, u32[]{:S(2)}) async-start(bf16[8,1,4]{2,1,0:T(2,128)(2,1)} %all_to_all.28), calls=%async_computation | async-start | bytes 8192 | tf_op jit(solution)/shard_map/all_to_all | solution.py:51
  51.4 10.7 %copy-start.1 = (u32[256]{0:T(256)S(1)}, u32[256]{0:T(256)}, u32[]{:S(2)}) copy-start(u32[256]{0:T(256)} %constant.24) | copy-start | bytes 3076
  51.4 304.2 %all-to-all-start.2 = ((bf16[32,32,4096]{2,1,0:T(8,128)(2,1)}), bf16[32,32,4096]{2,1,0:T(8,128)(2,1)}, u32[]{:S(2)}, u32[]{:S(2)}) async-start(bf16[32,32,4096]{2,1,0:T(8,128)(2,1)} %stack.3), calls=%async_computation.2 | async-start | bytes 16777216 | tf_op jit(solution)/shard_map/all_to_all | solution.py:63
  345.3 6.7 %copy-start.2 = (bf16[1024,4096]{1,0:T(8,128)(2,1)S(1)}, bf16[1024,4096]{1,0:T(8,128)(2,1)}, u32[]{:S(2)}) copy-start(bf16[1024,4096]{1,0:T(8,128)(2,1)} %all-gather.2.cloned.1.call-done) | copy-start | bytes 25165828
  345.3 6.8 %copy-start.3 = (bf16[1,224,4096]{2,1,0:T(8,128)(2,1)S(1)}, bf16[1,224,4096]{2,1,0:T(8,128)(2,1)}, u32[]{:S(2)}) copy-start(bf16[1,224,4096]{2,1,0:T(8,128)(2,1)} %param.12) | copy-start | bytes 5505028
  433.4 25.8 %all-to-all-start.4 = ((f32[8,1,4]{2,1,0:T(1,128)}), f32[8,1,4]{2,1,0:T(1,128)S(1)}, u32[]{:S(2)}, u32[]{:S(2)}) async-start(f32[8,1,4]{2,1,0:T(1,128)} %bitcast.11), calls=%async_computation.4 | async-start | bytes 8192 | tf_op jit(solution)/shard_map/all_to_all | solution.py:81
  438.4 7.2 %copy-start.4 = (f32[1024,224]{0,1:T(8,128)S(1)}, f32[1024,224]{0,1:T(8,128)}, u32[]{:S(2)}) copy-start(f32[1024,224]{0,1:T(8,128)} %fusion.8) | copy-start | bytes 2752516
  438.4 7.2 %copy-start.5 = (f32[1024,224]{0,1:T(8,128)S(1)}, f32[1024,224]{0,1:T(8,128)}, u32[]{:S(2)}) copy-start(f32[1024,224]{0,1:T(8,128)} %get-tuple-element.12) | copy-start | bytes 2752516
Sparse Core Ops, SparseCore 0:
  24.9 228.7 all-gather.1
